TPU v7x, 32 devices: a whole 2x2x4 slice. The times are simulated.
32 devices in a mesh: dp: 4 (over x, core), expert: 8 (over z, y).
Axes of the slice: x: 2, y: 2, z: 4, core: 2. Of those that a mesh axis runs over, the one named last changes fastest.
Arguments:
- tokens: bfloat16 [320, 4096], P('expert', 'dp'), may hold values from -6 to 6
- expert_ids: int32 [320, 8], P('expert'), may hold values from 0 to 15, all different within a row; in each aligned block of 320 rows (0 to 319, 320 to 639, ...) at most 240 rows name the same one
- routing_weights: bfloat16 [320, 8], P('expert'), may hold values from 0.049804688 to 0.29882812
- gate_weight: bfloat16 [16, 768, 4096], P('expert', None, 'dp'), may hold values from -0.09375 to 0.09375
- up_weight: bfloat16 [16, 768, 4096], P('expert', None, 'dp'), may hold values from -0.09375 to 0.09375
- down_weight: bfloat16 [16, 768, 4096], P('expert', None, 'dp'), may hold values from -0.21875 to 0.21875
- out_grad: bfloat16 [320, 4096], P('expert', 'dp'), may hold values from -1.5 to 1.5
Outputs:
- layer_out: bfloat16 [320, 4096], P('expert', 'dp')
- tokens_grad: bfloat16 [320, 4096], P('expert', 'dp')
- routing_grad: float32 [320, 8], P('expert')
- gate_weight_grad: bfloat16 [16, 768, 4096], P('expert', None, 'dp')
- up_weight_grad: bfloat16 [16, 768, 4096], P('expert', None, 'dp')
- down_weight_grad: bfloat16 [16, 768, 4096], P('expert', None, 'dp')
Inputs may be any that keep to these rules, and one draw needn't show every extreme that they name: `expert_ids`: each row names 8 different experts. No expert is named by more than 240 rows, a bound that some block reaches.
All inputs are finite; a program needn't handle non-finite values.
Results may differ from a plain program's by a relative error of at most 0.02.
Values may be sent and summed in bfloat16 or wider, within the bound.
A program may use at most 128 MiB of HBM per device.

v0:
```python
import jax
import jax.numpy as jnp
from jax import lax
from jax.sharding import PartitionSpec as P

TOP = 8
CAP = 240


def build_lists(ids_all, first_expert, expert_count):
    flat_ids = ids_all.reshape(-1)
    targets = first_expert + jnp.arange(expert_count, dtype=jnp.int32)
    matches = flat_ids[None, :] == targets[:, None]
    rank_pos = jnp.cumsum(matches.astype(jnp.int32), axis=1, dtype=jnp.int32) - 1
    target_pos = jnp.where(matches, rank_pos, CAP)
    slot_ids = jnp.broadcast_to(
        jnp.arange(flat_ids.shape[0], dtype=jnp.int32)[None, :], matches.shape
    )
    expert_row = jnp.broadcast_to(jnp.arange(expert_count, dtype=jnp.int32)[:, None], matches.shape)
    slot_lists = (
        jnp.zeros((expert_count, CAP), jnp.int32)
        .at[expert_row, target_pos]
        .set(slot_ids, mode="drop")
    )
    totals = jnp.sum(matches.astype(jnp.int32), axis=1, dtype=jnp.int32)
    is_live = jnp.arange(CAP, dtype=jnp.int32)[None, :] < totals[:, None]
    return (slot_lists.reshape(-1), is_live.reshape(-1))


def make_deltas(hidden_grad, gate_pre, up_pre):
    gate_sig = jax.nn.sigmoid(gate_pre)
    gate_delta = (hidden_grad * up_pre * gate_sig * (1.0 + gate_pre * (1.0 - gate_sig))).astype(
        jnp.bfloat16
    )
    up_delta = (hidden_grad * gate_pre * gate_sig).astype(jnp.bfloat16)
    return (gate_delta, up_delta)


def body(tokens, expert_ids, routing_weights, gate_weight, up_weight, down_weight, out_grad):
    expert_count = gate_weight.shape[0]
    hidden_width = gate_weight.shape[1]
    slice_width = tokens.shape[1]
    token_slice, weight_rows, grad_slice = (
        lax.all_gather(tokens, "expert", axis=0, tiled=True),
        lax.all_gather(routing_weights, "expert", axis=0, tiled=True),
        lax.all_gather(out_grad, "expert", axis=0, tiled=True),
    )
    ids_all = lax.all_gather(expert_ids, "expert", axis=0, tiled=True)
    token_total = token_slice.shape[0]
    first_expert = lax.axis_index("expert") * expert_count
    slot_lists, is_live = build_lists(ids_all, first_expert, expert_count)
    row_count = slot_lists.shape[0]
    token_index = slot_lists // TOP
    live_rows = is_live.astype(jnp.float32)
    row_acts = jnp.where(is_live[:, None], token_slice[token_index], jnp.zeros((), jnp.bfloat16))
    row_blocks = row_acts.reshape(expert_count, CAP, slice_width)
    gate_part = jnp.einsum(
        "ecd,efd->ecf", row_blocks, gate_weight, preferred_element_type=jnp.float32
    )
    up_part = jnp.einsum("ecd,efd->ecf", row_blocks, up_weight, preferred_element_type=jnp.float32)
    gate_part = gate_part.reshape(row_count, hidden_width)
    up_part = up_part.reshape(row_count, hidden_width)
    gate_pre, up_pre = (
        lax.psum(gate_part.astype(jnp.bfloat16), "dp").astype(jnp.float32),
        lax.psum(up_part.astype(jnp.bfloat16), "dp").astype(jnp.float32),
    )
    hidden = (jax.nn.silu(gate_pre) * up_pre).astype(jnp.bfloat16)
    hidden_blocks = hidden.reshape(expert_count, CAP, hidden_width)
    expert_out = jnp.einsum(
        "ecf,efd->ecd", hidden_blocks, down_weight, preferred_element_type=jnp.float32
    )
    expert_out = expert_out.reshape(row_count, slice_width)
    row_scale = weight_rows.reshape(-1)[slot_lists].astype(jnp.float32) * live_rows
    summed_rows = (
        jnp.zeros((token_total, slice_width), jnp.float32)
        .at[token_index]
        .add(expert_out * row_scale[:, None])
    )
    layer_out = lax.psum_scatter(
        summed_rows.astype(jnp.bfloat16), "expert", scatter_dimension=0, tiled=True
    )
    grad_rows = grad_slice[token_index].astype(jnp.float32)
    row_dots = jnp.sum(grad_rows * expert_out, axis=1) * live_rows
    scaled_grad = (grad_rows * row_scale[:, None]).astype(jnp.bfloat16)
    grad_blocks = scaled_grad.reshape(expert_count, CAP, slice_width)
    grad_part = jnp.einsum(
        "ecd,efd->ecf", grad_blocks, down_weight, preferred_element_type=jnp.float32
    )
    grad_part = grad_part.reshape(row_count, hidden_width)
    hidden_grad = lax.psum(grad_part.astype(jnp.bfloat16), "dp").astype(jnp.float32)
    gate_delta, up_delta = make_deltas(hidden_grad, gate_pre, up_pre)
    gate_delta = gate_delta.reshape(expert_count, CAP, hidden_width)
    up_delta = up_delta.reshape(expert_count, CAP, hidden_width)
    down_grad = jnp.einsum(
        "ecf,ecd->efd", hidden_blocks, grad_blocks, preferred_element_type=jnp.float32
    ).astype(jnp.bfloat16)
    gate_grad = jnp.einsum(
        "ecf,ecd->efd", gate_delta, row_blocks, preferred_element_type=jnp.float32
    ).astype(jnp.bfloat16)
    up_grad = jnp.einsum(
        "ecf,ecd->efd", up_delta, row_blocks, preferred_element_type=jnp.float32
    ).astype(jnp.bfloat16)
    row_terms = jnp.einsum(
        "ecf,efd->ecd", gate_delta, gate_weight, preferred_element_type=jnp.float32
    )
    row_terms = row_terms + jnp.einsum(
        "ecf,efd->ecd", up_delta, up_weight, preferred_element_type=jnp.float32
    )
    row_terms = row_terms.reshape(row_count, slice_width)
    input_rows = jnp.zeros((token_total, slice_width), jnp.float32).at[token_index].add(row_terms)
    dot_rows = (
        jnp.zeros((token_total * TOP,), jnp.float32)
        .at[slot_lists]
        .add(row_dots)
        .reshape(token_total, TOP)
    )
    input_col, dot_col = (
        lax.psum_scatter(
            input_rows.astype(jnp.bfloat16), "expert", scatter_dimension=0, tiled=True
        ).astype(jnp.float32),
        lax.psum_scatter(
            dot_rows.astype(jnp.bfloat16), "expert", scatter_dimension=0, tiled=True
        ).astype(jnp.float32),
    )
    routing_grad = lax.psum(dot_col, "dp")
    return (layer_out, input_col.astype(jnp.bfloat16), routing_grad, gate_grad, up_grad, down_grad)


def solution(mesh):
    in_specs = (
        P("expert", "dp"),
        P("expert", None),
        P("expert", None),
        P("expert", None, "dp"),
        P("expert", None, "dp"),
        P("expert", None, "dp"),
        P("expert", "dp"),
    )
    out_specs = (
        P("expert", "dp"),
        P("expert", "dp"),
        P("expert", None),
        P("expert", None, "dp"),
        P("expert", None, "dp"),
        P("expert", None, "dp"),
    )
    return jax.shard_map(body, mesh=mesh, in_specs=in_specs, out_specs=out_specs, check_vma=False)
```

profile of v0, /device:TPU:9, one launch (start us, length us, event | category | flops | bytes accessed | tf_op | source)
XLA Modules:
  0.0 429.4 jit_solution(16904763474245285972)
XLA Ops:
  7.3 22.0 %all-gather = s32[8,40,8]{1,2,0:T(8,128)S(1)} all-gather(s32[1,40,8]{1,2,0:T(8,128)} %bitcast.55), channel_id=1, replica_groups=mesh['dp'=4,'expert'=8] {'expert'}, dimensions={0}, use_global_device_ids=true | all-gather | bytes 11520 | tf_op jit(solution)/shard_map/all_gather | solution.py:48
  29.7 22.6 %all-gather.1 = bf16[8,40,8]{1,2,0:T(8,128)(2,1)S(1)} all-gather(bf16[1,40,8]{1,2,0:T(8,128)(2,1)} %bitcast.57), channel_id=1, replica_groups=mesh['dp'=4,'expert'=8] {'expert'}, dimensions={0}, use_global_device_ids=true | all-gather | bytes 5760 | tf_op jit(solution)/shard_map/all_gather | solution.py:45
  54.0 0.8 and_reduce_fusion
  54.8 0.8 multiply_reduce_fusion
  55.6 19.2 %scatter_custom_fusion.3 = s32[480]{0:T(512)S(1)} fusion(s32[5120]{0:T(1024)S(1)} %reshape.373, s32[5120]{0:T(1024)S(1)} %reshape.375, s32[]{:T(128)} %constant.17.clone.1), kind=kCustom, calls=%fused_computation.66 | custom fusion | bytes 1924
  74.9 3.5 gather_fusion.1
  78.6 26.8 %all_gather.13 = bf16[320,1024]{1,0:T(8,128)(2,1)} all-gather(bf16[40,1024]{1,0:T(8,128)(2,1)S(1)} %copy-done.12), channel_id=1, replica_groups=mesh['dp'=4,'expert'=8] {'expert'}, dimensions={0}, use_global_device_ids=true | all-gather | bytes 737280 | tf_op jit(solution)/shard_map/all_gather | solution.py:44
  105.4 27.6 %all_gather.15 = bf16[320,1024]{1,0:T(8,128)(2,1)} all-gather(bf16[40,1024]{1,0:T(8,128)(2,1)S(1)} %copy-done.13), channel_id=1, replica_groups=mesh['dp'=4,'expert'=8] {'expert'}, dimensions={0}, use_global_device_ids=true | all-gather | bytes 737280 | tf_op jit(solution)/shard_map/all_gather | solution.py:46
  133.1 4.6 %gather_fusion = bf16[480,1024]{1,0:T(8,128)(2,1)} fusion(bf16[320,1024]{1,0:T(8,128)(2,1)} %all_gather.13, s32[1024]{0:T(1024)S(1)} %pad_clamp_fusion.1), kind=kCustom, calls=%fused_computation | custom fusion | bytes 1968000 | tf_op jit(solution)/shard_map/gather | solution.py:55
  137.7 4.6 %gather_fusion.2 = bf16[480,1024]{1,0:T(8,128)(2,1)} fusion(bf16[320,1024]{1,0:T(8,128)(2,1)} %all_gather.15, s32[1024]{0:T(1024)S(1)} %pad_clamp_fusion.1), kind=kCustom, calls=%fused_computation.2 | custom fusion | bytes 1968000 | tf_op jit(solution)/shard_map/gather | solution.py:82
  142.3 4.2 convolution_convert_fusion.4
  146.5 1.9 convolution_convert_fusion.5
  148.5 2.0 convolution_convert_fusion.3
  150.8 77.9 %all-reduce.4.cloned.1.call-done = (bf16[480,768]{1,0:T(8,128)(2,1)}, bf16[480,768]{1,0:T(8,128)(2,1)}, bf16[480,768]{1,0:T(8,128)(2,1)}) async-done(((bf16[480,768]{1,0:T(8,128)(2,1)}, bf16[480,768]{1,0:T(8,128)(2,1)}, bf16[480,768]{1,0:T(8,128)(2,1)}), (bf16[480,768]{1,0:T(8,128)(2,1)}, bf16[480,768]{1,0:T(8,128)(2,1)}, bf16[480,768]{1,0:T(8,128)(2,1)})) %all-reduce.4.cloned.1.call-update) | async-done | bytes 2211856 | tf_op jit(solution)/shard_map/psum | solution.py:65
  228.7 3.5 fusion.11
  232.2 2.2 fusion.31
  234.4 2.3 fusion.1
  236.8 4.0 scatter_custom_fusion.2
  240.8 0.8 convert_element_type.118
  241.7 4.9 %convolution_add_fusion = f32[2,240,1024]{2,1,0:T(8,128)} fusion(f32[2,240,1024]{2,1,0:T(8,128)} %fusion.31, bf16[2,240,768]{2,1,0:T(8,128)(2,1)} %bitcast.43, bf16[2,768,1024]{2,1,0:T(8,128)(2,1)} %param.11), kind=kOutput, calls=%fused_computation.21 | convolution fusion | flops 755466240 | bytes 7815168 | tf_op jit(solution)/shard_map/ecf,efd->ecd/dot_general | solution.py:106
  246.6 6.5 %scatter_custom_fusion.1 = f32[320,1024]{1,0:T(8,128)} fusion(s32[480]{0:T(512)S(1)} %bitcast.50, f32[480,1024]{1,0:T(8,128)} %bitcast.45, f32[]{:T(128)} %constant.16.clone.1), kind=kCustom, calls=%fused_computation.36 | custom fusion | flops 491520 | bytes 1311232 | tf_op jit(solution)/shard_map/scatter-add | solution.py:110
  253.1 2.3 convert_element_type.116
  255.7 3.0 bitcast_multiply_fusion
  258.7 6.5 %scatter_custom_fusion = f32[320,1024]{1,0:T(8,128)} fusion(s32[480]{0:T(512)S(1)} %bitcast.51, f32[480,1024]{1,0:T(8,128)} %bitcast_multiply_fusion, f32[]{:T(128)} %constant.16.clone.1), kind=kCustom, calls=%fused_computation.38 | custom fusion | flops 491520 | bytes 1311232 | tf_op jit(solution)/shard_map/scatter-add | solution.py:77
  265.2 2.3 convert_element_type.105
  267.5 4.3 %convolution_convert_fusion.1 = bf16[2,768,1024]{2,1,0:T(8,128)(2,1)} fusion(bf16[2,240,768]{2,1,0:T(8,128)(2,1)} %bitcast.44, bf16[2,240,1024]{2,1,0:T(8,128)(2,1)} %bitcast.36, pred[2,240]{1,0:T(4,128)(4,1)S(1)} %iota_compare_fusion), kind=kOutput, calls=%fused_computation.14 | convolution fusion | flops 757039104 | bytes 4866528 | tf_op jit(solution)/shard_map/ecf,ecd->efd/dot_general | solution.py:100
  271.8 2.8 convolution_convert_fusion.2
  274.6 2.8 convolution_convert_fusion
  277.4 14.4 %reduce-scatter.10.cloned.1.call-done = bf16[40,8]{1,0:T(8,128)(2,1)} async-done(((bf16[320,8]{1,0:T(8,128)(2,1)}), bf16[40,8]{1,0:T(8,128)(2,1)}) %reduce-scatter.10.cloned.1.call-update) | async-done | bytes 656
  291.8 13.4 %psum.31 = f32[40,8]{1,0:T(8,128)S(1)} all-reduce(bf16[40,8]{1,0:T(8,128)(2,1)} %reduce-scatter.10.cloned.1.call-done), channel_id=1, replica_groups=mesh['dp'=4,'expert'=8] {'dp'}, use_global_device_ids=true, to_apply=%region_14.15 | all-reduce | flops 320 | bytes 1920 | tf_op jit(solution)/shard_map/psum | solution.py:125
  305.9 51.6 %reduce-scatter.8.cloned.1.call-done = bf16[40,1024]{1,0:T(8,128)(2,1)} async-done(((bf16[320,1024]{1,0:T(8,128)(2,1)}), bf16[40,1024]{1,0:T(8,128)(2,1)}) %reduce-scatter.8.cloned.1.call-update) | async-done | bytes 81936 | tf_op jit(solution)/shard_map/reduce_scatter | solution.py:118
  357.5 65.5 %reduce-scatter.6.cloned.1.call-done = bf16[40,1024]{1,0:T(8,128)(2,1)} async-done(((bf16[320,1024]{1,0:T(8,128)(2,1)}), bf16[40,1024]{1,0:T(8,128)(2,1)}) %reduce-scatter.6.cloned.1.call-update) | async-done | bytes 81936 | tf_op jit(solution)/shard_map/reduce_scatter | solution.py:79
  (66 shorter events, 3.9 us)
Async XLA Ops:
  7.2 141.3 %copy-start = (bf16[2,768,1024]{2,1,0:T(8,128)(2,1)S(1)}, bf16[2,768,1024]{2,1,0:T(8,128)(2,1)}, u32[]{:S(2)}) copy-start(bf16[2,768,1024]{2,1,0:T(8,128)(2,1)} %param.12) | copy-start | bytes 9437188
  7.2 71.4 %copy-start.12 = (bf16[40,1024]{1,0:T(8,128)(2,1)S(1)}, bf16[40,1024]{1,0:T(8,128)(2,1)}, u32[]{:S(2)}) copy-start(bf16[40,1024]{1,0:T(8,128)(2,1)} %param.7) | copy-start | bytes 245764
  7.2 98.3 %copy-start.13 = (bf16[40,1024]{1,0:T(8,128)(2,1)S(1)}, bf16[40,1024]{1,0:T(8,128)(2,1)}, u32[]{:S(2)}) copy-start(bf16[40,1024]{1,0:T(8,128)(2,1)} %param.13) | copy-start | bytes 245764
  7.2 221.5 %all-reduce.4.cloned.1.call-start = ((), (), s32[]{:S(2)}) async-start(), calls=%async_computation.6 | async-start | bytes 4423680 | tf_op jit(solution)/shard_map/psum | solution.py:65
  142.3 4.2 copy-start.4
  142.3 4.2 copy-start.10
  146.5 2.0 copy-start.1
  150.5 141.3 %reduce-scatter.10.cloned.1.call-start = ((), (), s32[]{:S(2)}) async-start(), calls=%async_computation.5 | async-start | bytes 92160
  228.7 3.5 copy-start.11
  232.2 2.2 copy-start.8
  232.2 2.2 copy-start.6
  232.2 2.2 copy-start.2
  241.6 115.8 %reduce-scatter.8.cloned.1.call-start = ((), (), s32[]{:S(2)}) async-start(), calls=%async_computation.4 | async-start | bytes 737280 | tf_op jit(solution)/shard_map/reduce_scatter | solution.py:118
  255.4 167.5 %reduce-scatter.6.cloned.1.call-start = ((), (), s32[]{:S(2)}) async-start(), calls=%async_computation.3 | async-start | bytes 737280 | tf_op jit(solution)/shard_map/reduce_scatter | solution.py:79
  267.5 4.3 %copy-start.5 = (bf16[480,1024]{1,0:T(8,128)(2,1)S(1)}, bf16[480,1024]{1,0:T(8,128)(2,1)}, u32[]{:S(2)}) copy-start(bf16[480,1024]{1,0:T(8,128)(2,1)} %gather_fusion) | copy-start | bytes 2949124
  267.5 4.3 %copy-start.9 = (bf16[480,768]{1,0:T(8,128)(2,1)S(1)}, bf16[480,768]{1,0:T(8,128)(2,1)}, u32[]{:S(2)}) copy-start(bf16[480,768]{1,0:T(8,128)(2,1)} %copy-done.8) | copy-start | bytes 2211844
  271.8 2.8 copy-start.3
  271.8 2.8 copy-start.7
Sparse Core Ops, SparseCore 0:
  150.6 78.0 all-reduce.3
  241.8 50.0 reduce-scatter.9
  295.7 61.7 reduce-scatter.7
  361.2 61.6 reduce-scatter.5
where the time goes:
time: 434 us; the launch traced here: 429 us
  waiting for transfers between devices  209 us (48%)
  blocking collectives  112 us (26%)
  local copies, waits for them, and re-layouts  34.6 us (8%)
  other arithmetic  31 us (7%)
  matrix products  27.4 us (6%)
  between operations  14 us (3%)
    psum x1, waiting for transfers between devices, body(): lax.psum(up_part.astype(jnp.bfloat16), 'dp').astype(jnp.float32)  77.9 us
    reduce_scatter x1, waiting for transfers between devices, body(): lax.psum_scatter(summed_rows.astype(jnp.bfloat16), 'expert', scatter_dime...  65.5 us
    reduce_scatter x1, waiting for transfers between devices, body(): lax.psum_scatter(input_rows.astype(jnp.bfloat16), 'expert', scatter_dimen...  51.6 us
    all_gather x1, blocking collectives, body(): lax.all_gather(out_grad, 'expert', axis=0, tiled=True)  27.6 us
    all_gather x1, blocking collectives, body(): lax.all_gather(tokens, 'expert', axis=0, tiled=True)  26.8 us
    all_gather x1, blocking collectives, body(): lax.all_gather(routing_weights, 'expert', axis=0, tiled=True)  22.6 us
    all_gather x1, blocking collectives, body(): ids_all = lax.all_gather(expert_ids, 'expert', axis=0, tiled=True)  22 us
    unnamed x31, local copies, waits for them, and re-layouts  20 us
  transfers between devices with their start and end apart: 4, of which 4 were waited for; matrix products, arithmetic and copies ran while one was open for 8% of the time, Pallas kernels for 0%

commit v1 on v0

v1 whole, which is shorter than its diff:
```python
import functools
import jax
import jax.numpy as jnp
from jax import lax
from jax.experimental import pallas as pl
from jax.experimental.pallas import tpu as pltpu
from jax.sharding import PartitionSpec as P

CAP = 240
F32 = jnp.float32
BF = jnp.bfloat16
VM = pl.BlockSpec(memory_space=pltpu.VMEM)


def factor(n):
    slow = 4 if n % 4 == 0 else n
    return slow, n // slow


def remote(src, dst, send, recv, where):
    return pltpu.make_async_remote_copy(
        src_ref=src, dst_ref=dst, send_sem=send, recv_sem=recv,
        device_id=where, device_id_type=pl.DeviceIdType.MESH,
    )


def greet(axis, n):
    me = lax.axis_index(axis)
    sem = pltpu.get_barrier_semaphore()
    for j in range(1, n):
        pl.semaphore_signal(sem, inc=1, device_id={axis: lax.rem(me + j, n)},
                            device_id_type=pl.DeviceIdType.MESH)
    pl.semaphore_wait(sem, n - 1)


def gather_kernel(n, *refs):
    k = 3
    ins, outs = refs[:k], refs[k:2 * k]
    up_s, up_r, dn_s, dn_r, side_s, side_r = refs[2 * k:]
    slow, fast = factor(n)
    me = lax.axis_index("expert")
    a, b = me // fast, lax.rem(me, fast)
    for i in range(k):
        outs[i][me] = ins[i][...]
    greet("expert", n)

    def hop(i, block, target, s_sem, r_sem, own):
        src = ins[i] if own else outs[i].at[block]
        return remote(src, outs[i].at[block], s_sem, r_sem, {"expert": target})

    def side(i, block, slot, j, own):
        return hop(i, block, a * fast + lax.rem(b + j, fast),
                   side_s.at[i, slot, j], side_r.at[i, slot, j], own)

    def up(i, s):
        return hop(i, (a - s) * fast + b, (a + 1) * fast + b, up_s.at[i, s], up_r.at[i, s], s == 0)

    def down(i, s):
        return hop(i, (a + s) * fast + b, (a - 1) * fast + b, dn_s.at[i, s], dn_r.at[i, s], s == 0)

    order = (2, 0, 1)
    for s in range(slow):
        if s > 0:
            for i in order:
                @pl.when(a - s >= 0)
                def _():
                    up(i, s - 1).wait_recv()

                @pl.when(a + s < slow)
                def _():
                    down(i, s - 1).wait_recv()
        if s < slow - 1:
            for i in order:
                @pl.when((a - s >= 0) & (a + 1 < slow))
                def _():
                    up(i, s).start()

                @pl.when((a + s < slow) & (a >= 1))
                def _():
                    down(i, s).start()
        for i in order:
            for j in range(1, fast):
                if s == 0:
                    side(i, me, 0, j, True).start()
                else:
                    @pl.when(a - s >= 0)
                    def _():
                        side(i, (a - s) * fast + b, s, j, False).start()

                    @pl.when(a + s < slow)
                    def _():
                        side(i, (a + s) * fast + b, slow - 1 + s, j, False).start()
    for i in order:
        for s in range(slow):
            if s < slow - 1:
                @pl.when((a - s >= 0) & (a + 1 < slow))
                def _():
                    up(i, s).wait_send()

                @pl.when((a + s < slow) & (a >= 1))
                def _():
                    down(i, s).wait_send()
            for j in range(1, fast):
                if s == 0:
                    side(i, me, 0, j, True).wait()
                else:
                    @pl.when(a - s >= 0)
                    def _():
                        side(i, (a - s) * fast + b, s, j, False).wait()

                    @pl.when(a + s < slow)
                    def _():
                        side(i, (a + s) * fast + b, slow - 1 + s, j, False).wait()


def gather_all(n, tok, grad, meta):
    ins = (tok, grad, meta)
    slow, fast = factor(n)
    dma = pltpu.SemaphoreType.DMA
    return pl.pallas_call(
        functools.partial(gather_kernel, n),
        out_shape=[jax.ShapeDtypeStruct((n,) + x.shape, x.dtype) for x in ins],
        in_specs=[VM] * 3,
        out_specs=[VM] * 3,
        scratch_shapes=[dma((3, slow))] * 4 + [dma((3, 2 * slow, fast))] * 2,
        compiler_params=pltpu.CompilerParams(collective_id=0, has_side_effects=True,
                                             vmem_limit_bytes=48 << 20),
    )(*ins)


def mix_kernel(n, ch, *refs):
    ins, outs = refs[:3], refs[3:6]
    got1, mine, got2, s1, r1, s2, r2, s3, r3, s4, r4 = refs[6:]
    m = n // 2
    me = lax.axis_index("dp")
    chip, core = me // 2, lax.rem(me, 2)
    greet("dp", n)
    partner = {"dp": chip * 2 + 1 - core}

    def pair(i, j, h):
        c = lax.rem(chip + j, m)
        seg = (c * 2 + 1 - core) * ch + h
        return remote(ins[i].at[seg], got1.at[i, j, h], s1.at[i, j, h], r1.at[i, j, h], partner)

    def cross(i, j, h):
        return remote(mine.at[i, j, h], got2.at[i, j, h], s2.at[i, j, h], r2.at[i, j, h],
                      {"dp": lax.rem(chip + j, m) * 2 + core})

    def spread(i, j, h):
        seg = me * ch + h
        return remote(outs[i].at[seg], outs[i].at[seg], s3.at[i, j, h], r3.at[i, j, h],
                      {"dp": lax.rem(chip + j, m) * 2 + core})

    def share(i, j, h):
        seg = (lax.rem(chip + m - j, m) * 2 + core) * ch + h
        return remote(outs[i].at[seg], outs[i].at[seg], s4.at[i, j, h], r4.at[i, j, h], partner)

    order = list(range(1, m)) + [0]
    for h in range(ch):
        for j in order:
            for i in range(3):
                pair(i, j, h).start()
    for h in range(ch):
        for j in order:
            for i in range(3):
                pair(i, j, h).wait_recv()
                seg = (lax.rem(chip + j, m) * 2 + core) * ch + h
                if j > 0:
                    mine[i, j, h] = (ins[i][seg].astype(F32) + got1[i, j, h].astype(F32)).astype(BF)
                    cross(i, j, h).start()
    for h in range(ch):
        total = []
        for i in range(3):
            v = ins[i][me * ch + h].astype(F32) + got1[i, 0, h].astype(F32)
            for j in range(1, m):
                cross(i, j, h).wait_recv()
                v = v + got2[i, j, h].astype(F32)
            total.append(v)
        gate, up, hg = total
        sig = jax.nn.sigmoid(gate)
        outs[0][me * ch + h] = (gate * sig * up).astype(BF)
        outs[1][me * ch + h] = (hg * up * sig * (1.0 + gate * (1.0 - sig))).astype(BF)
        outs[2][me * ch + h] = (hg * gate * sig).astype(BF)
        for i in range(3):
            for j in range(1, m):
                spread(i, j, h).start()
            share(i, 0, h).start()
    for h in range(ch):
        for j in range(1, m):
            for i in range(3):
                spread(i, j, h).wait_recv()
                share(i, j, h).start()
    for h in range(ch):
        for i in range(3):
            for j in range(m):
                pair(i, j, h).wait_send()
                share(i, j, h).wait()
                if j > 0:
                    cross(i, j, h).wait_send()
                    spread(i, j, h).wait_send()


def mix(n, gate, up, hg):
    rows, width = gate.shape
    ch = 3 if rows % (n * 3 * 8) == 0 else 1
    r = rows // (n * ch)
    ins = [x.reshape(n * ch, r, width) for x in (gate, up, hg)]
    m = n // 2
    dma = pltpu.SemaphoreType.DMA
    outs = pl.pallas_call(
        functools.partial(mix_kernel, n, ch),
        out_shape=[jax.ShapeDtypeStruct((n * ch, r, width), BF)] * 3,
        in_specs=[VM] * 3,
        out_specs=[VM] * 3,
        scratch_shapes=[pltpu.VMEM((3, m, ch, r, width), BF)] * 3 + [dma((3, m, ch))] * 8,
        compiler_params=pltpu.CompilerParams(collective_id=1, has_side_effects=True,
                                             vmem_limit_bytes=48 << 20),
    )(*ins)
    return [x.reshape(rows, width) for x in outs]


def reduce_kernel(n, nd, *refs):
    k = 3
    ins, outs = refs[:k], refs[k:2 * k]
    side_b, acc, up_b, dn_b, dots = refs[2 * k:3 * k], refs[3 * k:4 * k], refs[4 * k:5 * k], refs[5 * k:6 * k], refs[6 * k]
    side_s, side_r, up_s, up_r, dn_s, dn_r, dp_s, dp_r = refs[6 * k + 1:]
    slow, fast = factor(n)
    me = lax.axis_index("expert")
    dp = lax.axis_index("dp")
    a, b = me // fast, lax.rem(me, fast)
    sem = pltpu.get_barrier_semaphore()
    for j in range(1, n):
        pl.semaphore_signal(sem, inc=1, device_id={"expert": lax.rem(me + j, n)},
                            device_id_type=pl.DeviceIdType.MESH)
    for j in range(1, nd):
        pl.semaphore_signal(sem, inc=1, device_id={"dp": lax.rem(dp + j, nd)},
                            device_id_type=pl.DeviceIdType.MESH)
    pl.semaphore_wait(sem, n - 1 + nd - 1)

    def side(i, t, j):
        bb = lax.rem(b + j, fast)
        return remote(ins[i].at[t * fast + bb], side_b[i].at[t, j], side_s.at[i, t, j], side_r.at[i, t, j],
                      {"expert": a * fast + bb})

    def up(i, t):
        return remote(acc[i].at[t], up_b[i].at[t], up_s.at[i, t], up_r.at[i, t], {"expert": (a + 1) * fast + b})

    def down(i, t):
        return remote(acc[i].at[t], dn_b[i].at[t], dn_s.at[i, t], dn_r.at[i, t], {"expert": (a - 1) * fast + b})

    far = [t for d in range(slow) for t in ((slow - 1 - d, d) if slow - 1 - d > d else ((d,) if slow - 1 - d == d else ()))]
    for t in far:
        for i in range(k):
            for j in range(1, fast):
                side(i, t, j).start()
    for t in far:
        for i in range(k):
            v = ins[i][t * fast + b].astype(F32)
            for j in range(1, fast):
                side(i, t, j).wait_recv()
                v = v + side_b[i][t, j].astype(F32)
            acc[i][t] = v.astype(acc[i].dtype)

            @pl.when((t > a) & (a > 0))
            def _():
                up(i, t).wait_recv()
                acc[i][t] = (acc[i][t].astype(F32) + up_b[i][t].astype(F32)).astype(acc[i].dtype)

            @pl.when(t > a)
            def _():
                up(i, t).start()

            @pl.when((t < a) & (a < slow - 1))
            def _():
                down(i, t).wait_recv()
                acc[i][t] = (acc[i][t].astype(F32) + dn_b[i][t].astype(F32)).astype(acc[i].dtype)

            @pl.when(t < a)
            def _():
                down(i, t).start()

    def across(j):
        return remote(dots.at[0], dots.at[j], dp_s.at[j], dp_r.at[j], {"dp": lax.rem(dp + j, nd)})

    for i in (2, 0, 1):
        @pl.when(a > 0)
        def _():
            up(i, a).wait_recv()
            acc[i][a] = (acc[i][a].astype(F32) + up_b[i][a].astype(F32)).astype(acc[i].dtype)

        @pl.when(a < slow - 1)
        def _():
            down(i, a).wait_recv()
            acc[i][a] = (acc[i][a].astype(F32) + dn_b[i][a].astype(F32)).astype(acc[i].dtype)

        if i == 2:
            dots[0] = acc[2][a]
            for j in range(1, nd):
                across(j).start()
        else:
            outs[i][...] = acc[i][a]
    v = dots[0]
    for j in range(1, nd):
        across(j).wait()
        v = v + dots[j]
    outs[2][...] = v
    for t in range(slow):
        for i in range(k):
            for j in range(1, fast):
                side(i, t, j).wait_send()

            @pl.when(t > a)
            def _():
                up(i, t).wait_send()

            @pl.when(t < a)
            def _():
                down(i, t).wait_send()


def reduce_all(n, nd, out_rows, in_rows, dot_rows):
    ins = [x.reshape(n, x.shape[0] // n, x.shape[1]) for x in (out_rows, in_rows, dot_rows)]
    slow, fast = factor(n)
    dma = pltpu.SemaphoreType.DMA
    blocks = [(x.shape[1:], x.dtype) for x in ins]
    return pl.pallas_call(
        functools.partial(reduce_kernel, n, nd),
        out_shape=[jax.ShapeDtypeStruct(s, d) for s, d in blocks],
        in_specs=[VM] * 3,
        out_specs=[VM] * 3,
        scratch_shapes=[pltpu.VMEM((slow, fast) + s, d) for s, d in blocks]
        + [pltpu.VMEM((slow,) + s, d) for s, d in blocks] * 3
        + [pltpu.VMEM((nd,) + blocks[2][0], blocks[2][1])]
        + [dma((3, slow, fast))] * 2 + [dma((3, slow))] * 4 + [dma((nd,))] * 2,
        compiler_params=pltpu.CompilerParams(collective_id=2, has_side_effects=True,
                                             vmem_limit_bytes=48 << 20),
    )(*ins)


def body(n, nd, tokens, expert_ids, routing_weights, gate_weight, up_weight, down_weight, out_grad):
    e, f, d = gate_weight.shape
    top = expert_ids.shape[1]
    meta = jnp.concatenate([expert_ids.astype(F32), routing_weights.astype(F32)], axis=1)
    meta = jnp.pad(meta, ((0, 0), (0, 128 - 2 * top)))
    tok, grad, meta = gather_all(n, tokens, out_grad, meta)
    tok, grad = tok.reshape(-1, d), grad.reshape(-1, d)
    meta = meta.reshape(-1, 128)
    t = tok.shape[0]
    first = lax.axis_index("expert") * e
    targets = (first + jnp.arange(e, dtype=jnp.int32)).astype(F32)
    hit = meta[None, :, :top] == targets[:, None, None]
    match = jnp.any(hit, axis=2)
    weight = jnp.sum(jnp.where(hit, meta[None, :, top:2 * top], 0.0), axis=2)
    lower = (jnp.arange(t)[:, None] < jnp.arange(t)[None, :]).astype(BF)
    rank = jnp.dot(match.astype(BF), lower, preferred_element_type=F32).astype(jnp.int32)
    place = jnp.where(match, rank, CAP)
    pick = place[:, None, :] == jnp.arange(CAP, dtype=jnp.int32)[None, :, None]
    one = pick.astype(BF).reshape(e * CAP, t)
    scaled = jnp.where(pick, weight[:, None, :], 0.0).astype(BF).reshape(e * CAP, t)
    rows = jnp.dot(one, tok, preferred_element_type=F32).astype(BF).reshape(e, CAP, d)
    grows = jnp.dot(one, grad, preferred_element_type=F32).reshape(e, CAP, d)
    sgrad = jnp.dot(scaled, grad, preferred_element_type=F32).astype(BF).reshape(e, CAP, d)

    def ein(s, x, y):
        return jnp.einsum(s, x, y, preferred_element_type=F32)

    gate_part = ein("ecd,efd->ecf", rows, gate_weight).astype(BF).reshape(e * CAP, f)
    up_part = ein("ecd,efd->ecf", rows, up_weight).astype(BF).reshape(e * CAP, f)
    hg_part = ein("ecd,efd->ecf", sgrad, down_weight).astype(BF).reshape(e * CAP, f)
    hidden, gd, ud = [x.reshape(e, CAP, f) for x in mix(nd, gate_part, up_part, hg_part)]
    eo = ein("ecf,efd->ecd", hidden, down_weight)
    dots = jnp.sum(grows * eo, axis=2).astype(BF)
    dot_te = jnp.einsum("ect,ec->et", one.reshape(e, CAP, t), dots, preferred_element_type=F32)
    dot_rows = jnp.sum(jnp.where(hit, dot_te[:, :, None], 0.0), axis=0)
    dot_rows = jnp.pad(dot_rows, ((0, 0), (0, 128 - top)))
    out_rows = jnp.einsum("rt,rd->td", scaled, eo.reshape(e * CAP, d).astype(BF), preferred_element_type=F32).astype(BF)
    terms = (ein("ecf,efd->ecd", gd, gate_weight) + ein("ecf,efd->ecd", ud, up_weight)).astype(BF)
    in_rows = jnp.einsum("rt,rd->td", one, terms.reshape(e * CAP, d), preferred_element_type=F32).astype(BF)
    layer_out, tokens_grad, routing_grad = reduce_all(n, nd, out_rows, in_rows, dot_rows)
    down_grad = ein("ecf,ecd->efd", hidden, sgrad).astype(BF)
    gate_grad = ein("ecf,ecd->efd", gd, rows).astype(BF)
    up_grad = ein("ecf,ecd->efd", ud, rows).astype(BF)
    return layer_out, tokens_grad, routing_grad[:, :top], gate_grad, up_grad, down_grad


def solution(mesh):
    n, nd = mesh.shape["expert"], mesh.shape["dp"]
    w = P("expert", None, "dp")
    x = P("expert", "dp")
    r = P("expert", None)
    return jax.shard_map(functools.partial(body, n, nd), mesh=mesh, in_specs=(x, r, r, w, w, w, x),
                         out_specs=(x, x, r, w, w, w), check_vma=False)
```

time: 434 us -> 138 us (0.32)
  waiting for transfers between devices: 209 us -> 0 us
  blocking collectives: 112 us -> 0 us
  Pallas kernels: 0 us -> 85.9 us
  other arithmetic: 31 us -> 6.7 us
  local copies, waits for them, and re-layouts: 34.6 us -> 13.7 us
  between operations: 14 us -> 0.96 us
    reduce_scatter x2 -> x0, waiting for transfers between devices: 117 us -> none  [the longest x1 65.5 us: body(): lax.psum_scatter(summed_rows.astype(jnp.bfloat16), 'expert', scatter_dime...]
    all_gather x4 -> x0, blocking collectives: 99.1 us -> none  [the longest x1 27.6 us: body(): lax.all_gather(out_grad, 'expert', axis=0, tiled=True)]
    pallas_call x0 -> x3, Pallas kernels: none -> 85.9 us  [the longest x1 32.4 us: reduce_all(): pl.pallas_call(functools.partial(reduce_kernel, n, nd), out_shape=[jax.Sh...]
    psum x1 -> x0, waiting for transfers between devices: 77.9 us -> none  [body(): lax.psum(up_part.astype(jnp.bfloat16), 'dp').astype(jnp.float32)]
    scatter-add x3 -> x0, other arithmetic: 17 us -> none  [the longest x1 6.48 us: body(): jnp.zeros((token_total, slice_width), jnp.float32).at[token_index]]
    unnamed x5 -> x0, waiting for transfers between devices: 14.5 us -> none
    psum x1 -> x0, blocking collectives: 13.4 us -> none  [body(): routing_grad = lax.psum(dot_col, 'dp')]
    gather x3 -> x0, local copies, waits for them, and re-layouts: 12.8 us -> none  [the longest x1 4.62 us: body(): grad_rows = grad_slice[token_index].astype(jnp.float32)]
  transfers between devices with their start and end apart: 4 -> 0, of which waited for: 4 -> 0; matrix products, arithmetic and copies ran while one was open for 8% -> 0% of each run, Pallas kernels for 0% -> 0%
where the time goes in v1:
time: 138 us; the launch traced here: 137 us
  Pallas kernels  85.9 us (62%)
  matrix products  30 us (22%)
  local copies, waits for them, and re-layouts  13.7 us (10%)
  other arithmetic  6.7 us (5%)
    pallas_call x1, Pallas kernels, reduce_all(): pl.pallas_call(functools.partial(reduce_kernel, n, nd), out_shape=[jax.Sh...  32.4 us
    pallas_call x1, Pallas kernels, mix(): pl.pallas_call(functools.partial(mix_kernel, n, ch), out_shape=[jax.Shape...  32 us
    pallas_call x1, Pallas kernels, gather_all(): pl.pallas_call(functools.partial(gather_kernel, n), out_shape=[jax.ShapeD...  21.5 us
    dot_general x8, matrix products, ein(): return jnp.einsum(s, x, y, preferred_element_type=F32)  17.6 us
    unnamed x56, local copies, waits for them, and re-layouts  9.43 us
    dot_general x1, matrix products, body(): jnp.einsum('rt,rd->td', one, terms.reshape(e * CAP, d), preferred_element...  4.95 us
    dot_general x1, matrix products, body(): jnp.dot(one, tok, preferred_element_type=F32).astype(BF).reshape(e, CAP, d)  2.81 us

profile of v1, /device:TPU:9, one launch (start us, length us, event | category | flops | bytes accessed | tf_op | source)
XLA Modules:
  0.0 137.3 jit_solution(6728641750579100355)
XLA Ops:
  0.7 0.8 convert_element_type.77
  1.5 0.8 convert_element_type.78
  2.4 0.9 copy-done.10
  3.3 0.9 copy-done.11
  4.2 21.5 %shard_map.118 = (bf16[8,40,1024]{2,1,0:T(8,128)(2,1)S(1)}, bf16[8,40,1024]{2,1,0:T(8,128)(2,1)S(1)}, f32[8,40,128]{2,1,0:T(8,128)S(1)}) custom-call(bf16[40,1024]{1,0:T(8,128)(2,1)S(1)} %copy-done.10, bf16[40,1024]{1,0:T(8,128)(2,1)S(1)} %copy-done.11, f32[40,128]{1,0:T(8,128)S(1)} %pad.8.refs_2_), custom_call_target="tpu_custom_call" | custom-call | tf_op jit(solution)/shard_map/pallas_call | solution.py:120
  25.7 0.8 copy-done.5
  26.6 0.7 copy-done.12
  28.5 0.8 copy.31
  29.3 2.7 %select_convert_fusion = bf16[2,240,320]{1,0,2:T(2,128)(2,1)S(1)} fusion(bf16[2,320]{0,1:T(8,128)(2,1)S(1)} %copy.33, s32[2,320]{0,1:T(8,128)} %copy.31), kind=kLoop, calls=%fused_computation.18 | loop fusion | flops 307200 | bytes 311040 | tf_op jit(solution)/shard_map/convert_element_type | solution.py:359
  32.0 2.1 %iota_compare_fusion.1 = pred[2,240,320]{1,0,2:T(4,128)(4,1)} fusion(s32[2,320]{0,1:T(8,128)} %copy.31), kind=kLoop, calls=%fused_computation.19 | loop fusion | flops 153600 | bytes 156160 | tf_op jit(solution)/shard_map/eq | solution.py:357
  34.1 2.0 %copy.34 = pred[2,240,320]{2,1,0:T(8,128)(4,1)} copy(pred[2,240,320]{1,0,2:T(4,128)(4,1)} %iota_compare_fusion.1) | data formatting | bytes 307200 | tf_op jit(solution)/shard_map/eq | solution.py:357
  36.1 2.8 %convolution_convert_fusion.4 = bf16[480,1024]{1,0:T(8,128)(2,1)} fusion(pred[480,320]{1,0:T(8,128)(4,1)} %bitcast.86, bf16[320,1024]{1,0:T(8,128)(2,1)} %bitcast.79), kind=kOutput, calls=%fused_computation.6 | convolution fusion | flops 315064320 | bytes 1792000 | tf_op jit(solution)/shard_map/dot_general | solution.py:360
  38.9 0.9 convert_element_type.85
  39.8 2.0 %convolution_convert_fusion.3 = bf16[480,1024]{1,0:T(8,128)(2,1)S(1)} fusion(bf16[480,320]{0,1:T(8,128)(2,1)} %convert_element_type.85, bf16[320,1024]{1,0:T(8,128)(2,1)} %bitcast.67), kind=kOutput, calls=%fused_computation.5 | convolution fusion | flops 315064320 | bytes 1945600 | tf_op jit(solution)/shard_map/dot_general | solution.py:362
  41.9 1.1 convolution_convert_fusion.5
  43.0 1.1 convolution_convert_fusion.6
  44.2 0.7 copy-done.16
  44.9 1.0 convolution_convert_fusion.7
  45.9 32.0 %shard_map.119 = (bf16[12,40,768]{2,1,0:T(8,128)(2,1)S(1)}, bf16[12,40,768]{2,1,0:T(8,128)(2,1)S(1)}, bf16[12,40,768]{2,1,0:T(8,128)(2,1)S(1)}) custom-call(bf16[12,40,768]{2,1,0:T(8,128)(2,1)S(1)} %bitcast.74, bf16[12,40,768]{2,1,0:T(8,128)(2,1)S(1)} %bitcast.73, bf16[12,40,768]{2,1,0:T(8,128)(2,1)S(1)} %bitcast.72), custom_call_target="tpu_custom_call" | custom-call | tf_op jit(solution)/shard_map/pallas_call | solution.py:210
  78.0 0.9 fusion.13
  79.6 0.9 multiply_reduce_fusion
  80.5 1.4 %fusion = bf16[320,1024]{1,0:T(8,128)(2,1)} fusion(f32[2,240,1024]{2,1,0:T(8,128)S(1)} %fusion.13, bf16[2,240,320]{1,0,2:T(2,128)(2,1)S(1)} %select_convert_fusion), kind=kOutput, calls=%fused_computation.12 | convolution fusion | flops 315392000 | bytes 2928640 | tf_op jit(solution)/shard_map/rt,rd->td/dot_general | solution.py:376
  82.4 4.3 %convolution_convert_fusion = bf16[2,768,1024]{2,1,0:T(8,128)(2,1)} fusion(bf16[2,240,768]{2,1,0:T(8,128)(2,1)} %bitcast.66, bf16[2,240,1024]{2,1,0:T(8,128)(2,1)} %bitcast.85), kind=kOutput, calls=%fused_computation | convolution fusion | flops 756547584 | bytes 4866048 | tf_op jit(solution)/shard_map/ecf,ecd->efd/dot_general | solution.py:365
  86.7 2.2 %fusion.14 = f32[2,240,1024]{2,1,0:T(8,128)} fusion(bf16[2,240,768]{2,1,0:T(8,128)(2,1)S(1)} %bitcast.63, bf16[2,768,1024]{2,1,0:T(8,128)(2,1)S(1)} %copy-done.17), kind=kOutput, calls=%fused_computation.37 | convolution fusion | flops 754974720 | bytes 5849088 | tf_op jit(solution)/shard_map/ecf,efd->ecd/dot_general | solution.py:365
  88.9 4.9 %fusion.1 = bf16[320,1024]{1,0:T(8,128)(2,1)} fusion(pred[2,240,320]{2,1,0:T(8,128)(4,1)} %copy.34, f32[2,240,1024]{2,1,0:T(8,128)} %fusion.14, bf16[2,240,768]{2,1,0:T(8,128)(2,1)} %bitcast.70, bf16[2,768,1024]{2,1,0:T(8,128)(2,1)} %param.11), kind=kOutput, calls=%fused_computation.13 | convolution fusion | flops 1070858240 | bytes 6658048 | tf_op jit(solution)/shard_map/rt,rd->td/dot_general | solution.py:378
  93.8 1.1 copy-done.7
  94.9 1.1 copy-done.9
  96.0 32.4 %shard_map.120 = (bf16[40,1024]{1,0:T(8,128)(2,1)S(1)}, bf16[40,1024]{1,0:T(8,128)(2,1)S(1)}, f32[40,128]{1,0:T(8,128)S(1)}) custom-call(bf16[8,40,1024]{2,1,0:T(8,128)(2,1)S(1)} %bitcast.69, bf16[8,40,1024]{2,1,0:T(8,128)(2,1)S(1)} %bitcast.75, f32[8,40,128]{2,1,0:T(8,128)S(1)} %bitcast.77), custom_call_target="tpu_custom_call" | custom-call | tf_op jit(solution)/shard_map/pallas_call | solution.py:326
  128.4 0.7 copy.38
  129.0 4.2 %convolution_convert_fusion.1 = bf16[2,768,1024]{2,1,0:T(8,128)(2,1)} fusion(bf16[2,240,768]{2,1,0:T(8,128)(2,1)} %bitcast.71, bf16[2,240,1024]{2,1,0:T(8,128)(2,1)} %bitcast.80), kind=kOutput, calls=%fused_computation.1 | convolution fusion | flops 756547584 | bytes 4866048 | tf_op jit(solution)/shard_map/ecf,ecd->efd/dot_general | solution.py:365
  133.3 2.7 %convolution_convert_fusion.2 = bf16[2,768,1024]{2,1,0:T(8,128)(2,1)} fusion(bf16[2,240,768]{2,1,0:T(8,128)(2,1)S(1)} %bitcast.64, bf16[2,240,1024]{2,1,0:T(8,128)(2,1)S(1)} %bitcast.83), kind=kOutput, calls=%fused_computation.2 | convolution fusion | flops 756547584 | bytes 4866048 | tf_op jit(solution)/shard_map/ecf,ecd->efd/dot_general | solution.py:365
  136.0 0.6 copy.50
  (62 shorter events, 3.1 us)
Async XLA Ops:
  0.6 41.3 %copy-start = (bf16[2,768,1024]{2,1,0:T(8,128)(2,1)S(1)}, bf16[2,768,1024]{2,1,0:T(8,128)(2,1)}, u32[]{:S(2)}) copy-start(bf16[2,768,1024]{2,1,0:T(8,128)(2,1)} %param.12) | copy-start | bytes 9437188
  0.7 27.1 %copy-start.23 = (f32[2]{0:T(128)}, f32[2]{0:T(128)S(1)}, u32[]{:S(2)}) copy-start(f32[2]{0:T(128)S(1)} %add_convert_fusion.1) | copy-start | bytes 28
  2.4 0.9 copy-start.10
  3.3 0.9 copy-start.11
  25.7 0.8 copy-start.5
  26.5 0.8 copy-start.12
  27.5 0.6 copy-start.18
  27.9 0.6 copy-start.21
  39.8 3.2 %copy-start.13 = (bf16[480,1024]{1,0:T(8,128)(2,1)S(1)}, bf16[480,1024]{1,0:T(8,128)(2,1)}, u32[]{:S(2)}) copy-start(bf16[480,1024]{1,0:T(8,128)(2,1)} %convolution_convert_fusion.4) | copy-start | bytes 2949124
  39.8 3.2 %copy-start.25 = (bf16[2,768,1024]{2,1,0:T(8,128)(2,1)S(1)}, bf16[2,768,1024]{2,1,0:T(8,128)(2,1)}, u32[]{:S(2)}) copy-start(bf16[2,768,1024]{2,1,0:T(8,128)(2,1)} %param.11) | copy-start | bytes 9437188
  41.9 2.3 %copy-start.15 = (bf16[480,1024]{1,0:T(8,128)(2,1)}, bf16[480,1024]{1,0:T(8,128)(2,1)S(1)}, u32[]{:S(2)}) copy-start(bf16[480,1024]{1,0:T(8,128)(2,1)S(1)} %convolution_convert_fusion.3) | copy-start | bytes 2949124
  43.0 1.9 %copy-start.16 = (bf16[2,768,1024]{2,1,0:T(8,128)(2,1)S(1)}, bf16[2,768,1024]{2,1,0:T(8,128)(2,1)}, u32[]{:S(2)}) copy-start(bf16[2,768,1024]{2,1,0:T(8,128)(2,1)} %param.10) | copy-start | bytes 9437188
  78.0 2.5 %copy-start.1 = (bf16[12,40,768]{2,1,0:T(8,128)(2,1)}, bf16[12,40,768]{2,1,0:T(8,128)(2,1)S(1)}, u32[]{:S(2)}) copy-start(bf16[12,40,768]{2,1,0:T(8,128)(2,1)S(1)} %get-tuple-element.19) | copy-start | bytes 2211844
  78.0 2.5 %copy-start.4 = (bf16[12,40,768]{2,1,0:T(8,128)(2,1)}, bf16[12,40,768]{2,1,0:T(8,128)(2,1)S(1)}, u32[]{:S(2)}) copy-start(bf16[12,40,768]{2,1,0:T(8,128)(2,1)S(1)} %get-tuple-element.18) | copy-start | bytes 2211844
  78.0 2.5 %copy-start.8 = (bf16[12,40,768]{2,1,0:T(8,128)(2,1)}, bf16[12,40,768]{2,1,0:T(8,128)(2,1)S(1)}, u32[]{:S(2)}) copy-start(bf16[12,40,768]{2,1,0:T(8,128)(2,1)S(1)} %get-tuple-element.20) | copy-start | bytes 2211844
  78.0 1.6 %copy-start.6 = (bf16[8,40,1024]{2,1,0:T(8,128)(2,1)S(1)}, bf16[8,40,1024]{2,1,0:T(8,128)(2,1)}, u32[]{:S(2)}) copy-start(bf16[8,40,1024]{2,1,0:T(8,128)(2,1)} %copy-done.5) | copy-start | bytes 1966084
  78.0 1.6 %copy-start.22 = (s32[2,320]{1,0:T(2,128)S(1)}, s32[2,320]{1,0:T(2,128)}, u32[]{:S(2)}) copy-start(s32[2,320]{1,0:T(2,128)} %copy-done.21) | copy-start | bytes 7684
  79.6 2.4 %copy-start.20 = (pred[2,240,320]{2,1,0:T(8,128)(4,1)S(1)}, pred[2,240,320]{2,1,0:T(8,128)(4,1)}, u32[]{:S(2)}) copy-start(pred[2,240,320]{2,1,0:T(8,128)(4,1)} %copy.34) | copy-start | bytes 460804
  79.6 2.6 %copy-start.19 = (f32[320,8]{0,1:T(8,128)S(1)}, f32[320,8]{0,1:T(8,128)}, u32[]{:S(2)}) copy-start(f32[320,8]{0,1:T(8,128)} %copy-done.18) | copy-start | bytes 30724
  79.6 2.6 %copy-start.24 = (f32[2]{0:T(128)S(1)}, f32[2]{0:T(128)}, u32[]{:S(2)}) copy-start(f32[2]{0:T(128)} %copy-done.23) | copy-start | bytes 28
  82.3 4.3 %copy-start.2 = (bf16[12,40,768]{2,1,0:T(8,128)(2,1)S(1)}, bf16[12,40,768]{2,1,0:T(8,128)(2,1)}, u32[]{:S(2)}) copy-start(bf16[12,40,768]{2,1,0:T(8,128)(2,1)} %copy-done.1) | copy-start | bytes 2211844
  82.4 4.3 %copy-start.17 = (bf16[2,768,1024]{2,1,0:T(8,128)(2,1)S(1)}, bf16[2,768,1024]{2,1,0:T(8,128)(2,1)}, u32[]{:S(2)}) copy-start(bf16[2,768,1024]{2,1,0:T(8,128)(2,1)} %param.10) | copy-start | bytes 9437188
  93.8 1.1 copy-start.7
  94.9 1.1 copy-start.9
  129.0 4.3 %copy-start.3 = (bf16[12,40,768]{2,1,0:T(8,128)(2,1)S(1)}, bf16[12,40,768]{2,1,0:T(8,128)(2,1)}, u32[]{:S(2)}) copy-start(bf16[12,40,768]{2,1,0:T(8,128)(2,1)} %copy-done.1) | copy-start | bytes 2211844
  129.0 4.3 %copy-start.14 = (bf16[480,1024]{1,0:T(8,128)(2,1)S(1)}, bf16[480,1024]{1,0:T(8,128)(2,1)}, u32[]{:S(2)}) copy-start(bf16[480,1024]{1,0:T(8,128)(2,1)} %convolution_convert_fusion.4) | copy-start | bytes 2949124

commit v2 on v1

--- a/solution.py
+++ b/solution.py
@@ -337,6 +337,84 @@
     )(*ins)
 
 
+def dotted(x, y, dx, dy):
+    return lax.dot_general(x, y, (((dx,), (dy,)), ((), ())), preferred_element_type=F32)
+
+
+def rows_kernel(e, match_ref, weight_ref, tok_ref, grad_ref, one_ref, scaled_ref, rows_ref, grows_ref, sgrad_ref):
+    t = tok_ref.shape[0]
+    lower = (lax.broadcasted_iota(jnp.int32, (t, t), 0) < lax.broadcasted_iota(jnp.int32, (t, t), 1)).astype(F32)
+    match = match_ref[...]
+    rank = dotted(match.astype(BF), lower.astype(BF), 1, 0)
+    place = jnp.where(match > 0.5, rank, -1.0)
+    line = lax.broadcasted_iota(jnp.int32, (CAP, t), 0).astype(F32)
+    for i in range(e):
+        pick = jnp.abs(line - place[i:i + 1, :]) < 0.5
+        one = jnp.where(pick, 1.0, 0.0).astype(BF)
+        scaled = jnp.where(pick, weight_ref[i:i + 1, :], 0.0).astype(BF)
+        one_ref[i] = one
+        scaled_ref[i] = scaled
+        rows_ref[i] = dotted(one, tok_ref[...], 1, 0).astype(BF)
+        grows_ref[i] = dotted(one, grad_ref[...], 1, 0).astype(BF)
+        sgrad_ref[i] = dotted(scaled, grad_ref[...], 1, 0).astype(BF)
+
+
+def make_rows(match, weight, tok, grad):
+    e, t = match.shape
+    d = tok.shape[1]
+    pad = ((0, 16 - e), (0, 0))
+    pick = jax.ShapeDtypeStruct((e, CAP, t), BF)
+    wide = jax.ShapeDtypeStruct((e, CAP, d), BF)
+    return pl.pallas_call(
+        functools.partial(rows_kernel, e), out_shape=[pick, pick, wide, wide, wide],
+        in_specs=[VM] * 4, out_specs=[VM] * 5,
+        compiler_params=pltpu.CompilerParams(vmem_limit_bytes=48 << 20),
+    )(jnp.pad(match.astype(F32), pad), jnp.pad(weight, pad), tok, grad)
+
+
+def weight_kernel(hid, gd, ud, rows, sgrad, gate_o, up_o, down_o):
+    gate_o[0] = dotted(gd[0], rows[0], 0, 0).astype(BF)
+    up_o[0] = dotted(ud[0], rows[0], 0, 0).astype(BF)
+    down_o[0] = dotted(hid[0], sgrad[0], 0, 0).astype(BF)
+
+
+def weight_grads(hidden, gd, ud, rows, sgrad):
+    e, c, f = hidden.shape
+    d = rows.shape[2]
+    fb = 256 if f % 256 == 0 else f
+    narrow = pl.BlockSpec((1, c, fb), lambda i, j: (i, 0, j))
+    whole = pl.BlockSpec((1, c, d), lambda i, j: (i, 0, 0))
+    out = pl.BlockSpec((1, fb, d), lambda i, j: (i, j, 0))
+    return pl.pallas_call(
+        weight_kernel, grid=(e, f // fb), out_shape=[jax.ShapeDtypeStruct((e, f, d), BF)] * 3,
+        in_specs=[narrow] * 3 + [whole] * 2, out_specs=[out] * 3,
+        compiler_params=pltpu.CompilerParams(vmem_limit_bytes=48 << 20),
+    )(hidden, gd, ud, rows, sgrad)
+
+
+def back_kernel(e, gd, ud, gw, uw, one, out):
+    total = None
+    for i in range(e):
+        terms = (dotted(gd[i], gw[i], 1, 0) + dotted(ud[i], uw[i], 1, 0)).astype(BF)
+        part = dotted(one[i], terms, 0, 0)
+        total = part if total is None else total + part
+    out[...] = total.astype(BF)
+
+
+def back_rows(gd, ud, gate_weight, up_weight, one):
+    e, f, d = gate_weight.shape
+    t = one.shape[2]
+    db = 256 if d % 256 == 0 else d
+    delta = pl.BlockSpec(gd.shape, lambda j: (0, 0, 0))
+    w = pl.BlockSpec((e, f, db), lambda j: (0, 0, j))
+    return pl.pallas_call(
+        functools.partial(back_kernel, e), grid=(d // db,), out_shape=jax.ShapeDtypeStruct((t, d), BF),
+        in_specs=[delta, delta, w, w, pl.BlockSpec(one.shape, lambda j: (0, 0, 0))],
+        out_specs=pl.BlockSpec((t, db), lambda j: (0, j)),
+        compiler_params=pltpu.CompilerParams(vmem_limit_bytes=48 << 20),
+    )(gd, ud, gate_weight, up_weight, one)
+
+
 def body(n, nd, tokens, expert_ids, routing_weights, gate_weight, up_weight, down_weight, out_grad):
     e, f, d = gate_weight.shape
     top = expert_ids.shape[1]
@@ -351,15 +429,7 @@
     hit = meta[None, :, :top] == targets[:, None, None]
     match = jnp.any(hit, axis=2)
     weight = jnp.sum(jnp.where(hit, meta[None, :, top:2 * top], 0.0), axis=2)
-    lower = (jnp.arange(t)[:, None] < jnp.arange(t)[None, :]).astype(BF)
-    rank = jnp.dot(match.astype(BF), lower, preferred_element_type=F32).astype(jnp.int32)
-    place = jnp.where(match, rank, CAP)
-    pick = place[:, None, :] == jnp.arange(CAP, dtype=jnp.int32)[None, :, None]
-    one = pick.astype(BF).reshape(e * CAP, t)
-    scaled = jnp.where(pick, weight[:, None, :], 0.0).astype(BF).reshape(e * CAP, t)
-    rows = jnp.dot(one, tok, preferred_element_type=F32).astype(BF).reshape(e, CAP, d)
-    grows = jnp.dot(one, grad, preferred_element_type=F32).reshape(e, CAP, d)
-    sgrad = jnp.dot(scaled, grad, preferred_element_type=F32).astype(BF).reshape(e, CAP, d)
+    one, scaled, rows, grows, sgrad = make_rows(match, weight, tok, grad)
 
     def ein(s, x, y):
         return jnp.einsum(s, x, y, preferred_element_type=F32)
@@ -369,17 +439,14 @@
     hg_part = ein("ecd,efd->ecf", sgrad, down_weight).astype(BF).reshape(e * CAP, f)
     hidden, gd, ud = [x.reshape(e, CAP, f) for x in mix(nd, gate_part, up_part, hg_part)]
     eo = ein("ecf,efd->ecd", hidden, down_weight)
-    dots = jnp.sum(grows * eo, axis=2).astype(BF)
-    dot_te = jnp.einsum("ect,ec->et", one.reshape(e, CAP, t), dots, preferred_element_type=F32)
+    dots = jnp.sum(grows.astype(F32) * eo, axis=2).astype(BF)
+    dot_te = jnp.einsum("ect,ec->et", one, dots, preferred_element_type=F32)
     dot_rows = jnp.sum(jnp.where(hit, dot_te[:, :, None], 0.0), axis=0)
     dot_rows = jnp.pad(dot_rows, ((0, 0), (0, 128 - top)))
-    out_rows = jnp.einsum("rt,rd->td", scaled, eo.reshape(e * CAP, d).astype(BF), preferred_element_type=F32).astype(BF)
-    terms = (ein("ecf,efd->ecd", gd, gate_weight) + ein("ecf,efd->ecd", ud, up_weight)).astype(BF)
-    in_rows = jnp.einsum("rt,rd->td", one, terms.reshape(e * CAP, d), preferred_element_type=F32).astype(BF)
+    out_rows = jnp.einsum("rt,rd->td", scaled.reshape(e * CAP, t), eo.reshape(e * CAP, d).astype(BF), preferred_element_type=F32).astype(BF)
+    in_rows = back_rows(gd, ud, gate_weight, up_weight, one)
     layer_out, tokens_grad, routing_grad = reduce_all(n, nd, out_rows, in_rows, dot_rows)
-    down_grad = ein("ecf,ecd->efd", hidden, sgrad).astype(BF)
-    gate_grad = ein("ecf,ecd->efd", gd, rows).astype(BF)
-    up_grad = ein("ecf,ecd->efd", ud, rows).astype(BF)
+    gate_grad, up_grad, down_grad = weight_grads(hidden, gd, ud, rows, sgrad)
     return layer_out, tokens_grad, routing_grad[:, :top], gate_grad, up_grad, down_grad
 
 

time: 138 us -> 128 us (0.928)
  matrix products: 30 us -> 5.61 us
  Pallas kernels: 85.9 us -> 98.8 us
  local copies, waits for them, and re-layouts: 13.7 us -> 20.4 us
  other arithmetic: 6.7 us -> 1.92 us
    dot_general x8 -> x4, matrix products: 17.6 us -> 4.91 us  [ein(): return jnp.einsum(s, x, y, preferred_element_type=F32)]
    pallas_call x0 -> x3, Pallas kernels: none -> 12.7 us  [the longest x1 5.55 us: weight_grads(): pl.pallas_call(weight_kernel, grid=(e, f // fb), out_shape=[jax.ShapeDtyp...]
    dot_general x7 -> x2, matrix products: 12.4 us -> 0.69 us  [the longest x1 0.52 us: body(): jnp.einsum('rt,rd->td', scaled.reshape(e * CAP, t), eo.reshape(e * CAP, d...]
    unnamed x56 -> x54, local copies, waits for them, and re-layouts: 9.43 us -> 19.1 us
    convert_element_type x1 -> x0, other arithmetic: 2.73 us -> none  [body(): jnp.where(pick, weight[:, None, :], 0.0).astype(BF).reshape(e * CAP, t)]
    eq x1 -> x0, other arithmetic: 2.07 us -> none  [body(): pick = place[:, None, :] == jnp.arange(CAP, dtype=jnp.int32)[None, :, None]]
    eq x1 -> x0, local copies, waits for them, and re-layouts: 1.96 us -> none  [body(): pick = place[:, None, :] == jnp.arange(CAP, dtype=jnp.int32)[None, :, None]]
where the time goes in v2:
time: 128 us
  Pallas kernels  98.8 us (77%)
  local copies, waits for them, and re-layouts  20.4 us (16%)
  matrix products  5.61 us (4%)
  other arithmetic  1.92 us (2%)
    pallas_call x1, Pallas kernels, reduce_all(): pl.pallas_call(functools.partial(reduce_kernel, n, nd), out_shape=[jax.Sh...  32.6 us
    pallas_call x1, Pallas kernels, mix(): pl.pallas_call(functools.partial(mix_kernel, n, ch), out_shape=[jax.Shape...  32 us
    pallas_call x1, Pallas kernels, gather_all(): pl.pallas_call(functools.partial(gather_kernel, n), out_shape=[jax.ShapeD...  21.5 us
    unnamed x54, local copies, waits for them, and re-layouts  19.1 us
    pallas_call x1, Pallas kernels, weight_grads(): pl.pallas_call(weight_kernel, grid=(e, f // fb), out_shape=[jax.ShapeDtyp...  5.55 us
    pallas_call x1, Pallas kernels, back_rows(): pl.pallas_call(functools.partial(back_kernel, e), grid=(d // db,), out_sh...  5.25 us
    dot_general x4, matrix products, ein(): return jnp.einsum(s, x, y, preferred_element_type=F32)  4.91 us

profile of v2, /device:TPU:9, one launch (start us, length us, event | category | flops | bytes accessed | tf_op | source)
XLA Modules:
  0.0 127.7 jit_solution(17176919799683309795)
XLA Ops:
  0.7 0.8 convert_element_type.43
  1.5 0.8 convert_element_type.44
  2.4 0.9 copy-done.21
  3.3 0.9 copy-done.22
  4.2 21.5 %shard_map.118 = (bf16[8,40,1024]{2,1,0:T(8,128)(2,1)S(1)}, bf16[8,40,1024]{2,1,0:T(8,128)(2,1)S(1)}, f32[8,40,128]{2,1,0:T(8,128)S(1)}) custom-call(bf16[40,1024]{1,0:T(8,128)(2,1)S(1)} %copy-done.21, bf16[40,1024]{1,0:T(8,128)(2,1)S(1)} %copy-done.22, f32[40,128]{1,0:T(8,128)S(1)} %pad.17.refs_2_), custom_call_target="tpu_custom_call" | custom-call | tf_op jit(solution)/shard_map/pallas_call | solution.py:120
  25.7 0.8 copy-done.15
  26.5 0.8 copy-done.17
  27.9 1.1 copy-done.16
  29.0 1.1 copy-done.18
  30.1 1.9 %shard_map.119 = (bf16[2,240,320]{2,1,0:T(8,128)(2,1)S(1)}, bf16[2,240,320]{2,1,0:T(8,128)(2,1)S(1)}, bf16[2,240,1024]{2,1,0:T(8,128)(2,1)S(1)}, bf16[2,240,1024...) custom-call(f32[16,320]{1,0:T(8,128)S(1)} %pad_convert_fusion.match_ref, f32[16,320]{1,0:T(8,128)S(1)} %pad.20.weight_ref, ...), custom_call_target="tpu_custom_call" | custom-call | tf_op jit(solution)/shard_map/pallas_call | solution.py:368
  32.0 1.0 convolution_convert_fusion
  33.0 1.0 convolution_convert_fusion.1
  34.1 0.8 copy-done.1
  34.9 1.0 convolution_convert_fusion.2
  35.9 32.0 %shard_map.120 = (bf16[12,40,768]{2,1,0:T(8,128)(2,1)S(1)}, bf16[12,40,768]{2,1,0:T(8,128)(2,1)S(1)}, bf16[12,40,768]{2,1,0:T(8,128)(2,1)S(1)}) custom-call(bf16[12,40,768]{2,1,0:T(8,128)(2,1)S(1)} %bitcast.44, bf16[12,40,768]{2,1,0:T(8,128)(2,1)S(1)} %bitcast.43, bf16[12,40,768]{2,1,0:T(8,128)(2,1)S(1)} %bitcast.42), custom_call_target="tpu_custom_call" | custom-call | tf_op jit(solution)/shard_map/pallas_call | solution.py:210
  68.0 1.9 %multiply_reduce_fusion = (bf16[2,240]{1,0:T(2,128)(2,1)S(1)}, bf16[2,240,1024]{2,1,0:T(8,128)(2,1)}) fusion(bf16[2,240,1024]{2,1,0:T(8,128)(2,1)S(1)} %get-tuple-element.33, bf16[2,240,768]{2,1,0:T(8,128)(2,1)S(1)} %bitcast.40, bf16[2,768,1024]{2,1,0:T(8,128)(2,1)S(1)} %copy-done), kind=kOutput, calls=%fused_computation | convolution fusion | flops 756940288 | bytes 5850048 | tf_op jit(solution)/shard_map/ecf,efd->ecd/dot_general | solution.py:435
  70.1 0.8 copy.29
  70.9 0.9 pad.21.clone
  71.9 1.9 %copy-done.2 = bf16[2,768,1024]{2,1,0:T(8,128)(2,1)S(1)} copy-done((bf16[2,768,1024]{2,1,0:T(8,128)(2,1)S(1)}, bf16[2,768,1024]{2,1,0:T(8,128)(2,1)}, u32[]{:S(2)}) %copy-start.2) | copy-done | bytes 3145752
  73.8 1.1 copy-done.4
  74.9 1.1 copy-done.7
  76.0 5.2 %shard_map.121 = bf16[320,1024]{1,0:T(8,128)(2,1)S(1)} custom-call(bf16[2,240,768]{2,1,0:T(8,128)(2,1)S(1)} %bitcast.34, bf16[2,240,768]{2,1,0:T(8,128)(2,1)S(1)} %bitcast.36, bf16[2,768,1024]{2,1,0:T(8,128)(2,1)S(1)} %copy-done.2, bf16[2,768,1024]{2,1,0:T(8,128)(2,1)} %uw.1, bf16[2,240,320]{2,1,0:T(8,128)(2,1)S(1)} %get-tuple-element.32.one), custom_call_target="tpu_custom_call" | custom-call | tf_op jit(solution)/shard_map/pallas_call | solution.py:410
  81.8 32.6 %shard_map.122 = (bf16[40,1024]{1,0:T(8,128)(2,1)S(1)}, bf16[40,1024]{1,0:T(8,128)(2,1)S(1)}, f32[40,128]{1,0:T(8,128)S(1)}) custom-call(bf16[8,40,1024]{2,1,0:T(8,128)(2,1)S(1)} %bitcast.39, bf16[8,40,1024]{2,1,0:T(8,128)(2,1)S(1)} %bitcast.38, f32[8,40,128]{2,1,0:T(8,128)S(1)} %bitcast.48), custom_call_target="tpu_custom_call" | custom-call | tf_op jit(solution)/shard_map/pallas_call | solution.py:326
  114.4 0.7 copy.25
  115.1 1.1 copy-done.5
  116.2 1.1 copy-done.8
  117.3 1.2 copy-done.10
  118.5 1.2 copy-done.12
  119.7 1.1 copy-done.14
  120.9 5.5 %shard_map.123 = (bf16[2,768,1024]{2,1,0:T(8,128)(2,1)}, bf16[2,768,1024]{2,1,0:T(8,128)(2,1)}, bf16[2,768,1024]{2,1,0:T(8,128)(2,1)}) custom-call(bf16[2,240,768]{2,1,0:T(8,128)(2,1)S(1)} %bitcast.41, bf16[2,240,768]{2,1,0:T(8,128)(2,1)S(1)} %bitcast.35, bf16[2,240,768]{2,1,0:T(8,128)(2,1)S(1)} %bitcast.37, bf16[2,240,1024]{2,1,0:T(8,128)(2,1)S(1)} %copy-done.10, ...), custom_call_target="tpu_custom_call" | custom-call | tf_op jit(solution)/shard_map/pallas_call | solution.py:388
  126.4 0.6 copy.36
  127.0 0.6 copy.37
  (50 shorter events, 1.5 us)
Async XLA Ops:
  0.6 31.3 %copy-start = (bf16[2,768,1024]{2,1,0:T(8,128)(2,1)S(1)}, bf16[2,768,1024]{2,1,0:T(8,128)(2,1)}, u32[]{:S(2)}) copy-start(bf16[2,768,1024]{2,1,0:T(8,128)(2,1)} %param.12) | copy-start | bytes 9437188
  2.4 0.9 copy-start.21
  3.3 0.9 copy-start.22
  25.7 0.8 copy-start.15
  26.5 0.8 copy-start.17
  27.9 1.1 copy-start.16
  29.0 1.1 copy-start.18
  30.0 3.0 %copy-start.23 = (bf16[2,768,1024]{2,1,0:T(8,128)(2,1)S(1)}, bf16[2,768,1024]{2,1,0:T(8,128)(2,1)}, u32[]{:S(2)}) copy-start(bf16[2,768,1024]{2,1,0:T(8,128)(2,1)} %uw.1) | copy-start | bytes 9437188
  31.9 1.1 copy-start.19
  31.9 2.1 %copy-start.11 = (bf16[2,240,1024]{2,1,0:T(8,128)(2,1)}, bf16[2,240,1024]{2,1,0:T(8,128)(2,1)S(1)}, u32[]{:S(2)}) copy-start(bf16[2,240,1024]{2,1,0:T(8,128)(2,1)S(1)} %get-tuple-element.28.sgrad) | copy-start | bytes 2949124
  32.0 2.1 %copy-start.9 = (bf16[2,240,1024]{2,1,0:T(8,128)(2,1)}, bf16[2,240,1024]{2,1,0:T(8,128)(2,1)S(1)}, u32[]{:S(2)}) copy-start(bf16[2,240,1024]{2,1,0:T(8,128)(2,1)S(1)} %get-tuple-element.27.rows) | copy-start | bytes 2949124
  33.0 1.9 %copy-start.1 = (bf16[2,768,1024]{2,1,0:T(8,128)(2,1)S(1)}, bf16[2,768,1024]{2,1,0:T(8,128)(2,1)}, u32[]{:S(2)}) copy-start(bf16[2,768,1024]{2,1,0:T(8,128)(2,1)} %gw.1) | copy-start | bytes 9437188
  67.9 2.1 %copy-start.3 = (bf16[12,40,768]{2,1,0:T(8,128)(2,1)}, bf16[12,40,768]{2,1,0:T(8,128)(2,1)S(1)}, u32[]{:S(2)}) copy-start(bf16[12,40,768]{2,1,0:T(8,128)(2,1)S(1)} %get-tuple-element.30) | copy-start | bytes 2211844
  67.9 2.1 %copy-start.6 = (bf16[12,40,768]{2,1,0:T(8,128)(2,1)}, bf16[12,40,768]{2,1,0:T(8,128)(2,1)S(1)}, u32[]{:S(2)}) copy-start(bf16[12,40,768]{2,1,0:T(8,128)(2,1)S(1)} %get-tuple-element.31) | copy-start | bytes 2211844
  68.0 2.1 %copy-start.13 = (bf16[12,40,768]{2,1,0:T(8,128)(2,1)}, bf16[12,40,768]{2,1,0:T(8,128)(2,1)S(1)}, u32[]{:S(2)}) copy-start(bf16[12,40,768]{2,1,0:T(8,128)(2,1)S(1)} %get-tuple-element.29) | copy-start | bytes 2211844
  71.9 1.9 %copy-start.2 = (bf16[2,768,1024]{2,1,0:T(8,128)(2,1)S(1)}, bf16[2,768,1024]{2,1,0:T(8,128)(2,1)}, u32[]{:S(2)}) copy-start(bf16[2,768,1024]{2,1,0:T(8,128)(2,1)} %gw.1) | copy-start | bytes 9437188
  73.8 1.1 copy-start.4
  74.9 1.1 copy-start.7
  76.0 5.3 %copy-start.20 = (bf16[2,240,320]{2,1,0:T(8,128)(2,1)S(1)}, bf16[2,240,320]{2,1,0:T(8,128)(2,1)}, u32[]{:S(2)}) copy-start(bf16[2,240,320]{2,1,0:T(8,128)(2,1)} %copy-done.19) | copy-start | bytes 921604
  76.0 5.3 %copy-start.24 = (bf16[2,240,1024]{2,1,0:T(8,128)(2,1)S(1)}, bf16[2,240,1024]{2,1,0:T(8,128)(2,1)}, u32[]{:S(2)}) copy-start(bf16[2,240,1024]{2,1,0:T(8,128)(2,1)} %get-tuple-element.61) | copy-start | bytes 2949124
  115.1 1.1 copy-start.5
  116.2 1.1 copy-start.8
  117.3 1.2 copy-start.10
  118.5 1.2 copy-start.12
  119.7 1.1 copy-start.14
